TPU v7x, 256 devices: a whole 4x4x8 slice. The times are simulated.
256 devices in a mesh: scen: 16 (over y, x), blk: 16 (over z, core).
Axes of the slice: x: 4, y: 4, z: 8, core: 2. Of those that a mesh axis runs over, the one named last changes fastest.
Arguments:
- link: bfloat16 [64, 256, 4096], P('scen', None, 'blk'), may hold values from -0.15625 to 0.15625
- leaf_inverse: bfloat16 [64, 256, 256], P('scen'), as said below
- leaf_rhs: float32 [64, 256], P('scen'), may hold values from -6 to 6
- node_rhs: float32 [2, 4096], P(None, 'blk'), may hold values from -6 to 6
- node_diag: float32 [2, 4096], P(None, 'blk'), may hold values from 0.5 to 4
- parent: int32 [64], P('scen'), may hold values from 0 to 1
- tile_mask: int32 [64, 16], P('scen', 'blk'), may hold values 0 or 1
Outputs:
- node_solution: float32 [2, 4096], P(None, 'blk')
- leaf_solution: float32 [64, 256], P('scen')
- schur: float32 [2, 4096, 4096], P(None, 'blk', 'scen')
Inputs may be any that keep to these rules, and one draw needn't show every extreme that they name: `leaf_inverse`: its diagonal entries lie within 1 to 2.
All inputs are finite; a program needn't handle non-finite values. No bound on the sum of `tile_mask` on one device may be relied on, other than what follows from the above.
Results may differ from a plain program's by a relative error of at most 0.0017.
Values may be sent and summed in bfloat16 or wider, within the bound.
A program may use at most 128 MiB of HBM per device.

v0:
```python
import jax
import jax.numpy as jnp
from jax import lax
from jax.sharding import PartitionSpec as P

ITERS = 4
highest = lax.Precision.HIGHEST
damping = 0.4


def body(link, leaf_inverse, leaf_rhs, node_rhs, node_diag, parent, tile_mask):
    leaf_count, width_leaf, tile_width = link.shape
    node_count = node_rhs.shape[0]
    scen_count = lax.axis_size("scen")
    blk_count = lax.axis_size("blk")
    full_width = tile_width * blk_count
    scen_index = lax.axis_index("scen")
    blk_index = lax.axis_index("blk")
    node_ids = lax.broadcasted_iota(jnp.int32, (leaf_count, node_count), 1)
    member = parent[:, None] == node_ids
    member_f = member.astype(jnp.float32)
    masked = link * tile_mask.astype(jnp.bfloat16)[:, :, None]
    solved = jnp.einsum(
        "lnm,lmc->lnc", leaf_inverse, masked, preferred_element_type=jnp.float32
    ).astype(jnp.bfloat16)
    chosen = masked[None] * member.astype(jnp.bfloat16).T[:, :, None, None]
    chosen = chosen.reshape(node_count, leaf_count * width_leaf, tile_width)
    portion = lax.all_gather(solved, "blk", axis=2, tiled=True)
    stacked = portion.reshape(leaf_count * width_leaf, portion.shape[2])
    partial_value = jnp.einsum("pkr,kc->prc", chosen, stacked, preferred_element_type=jnp.float32)
    diagonal_tile = lax.dynamic_slice_in_dim(partial_value, blk_index * tile_width, tile_width, 2)
    diag_terms = jnp.diagonal(diagonal_tile, axis1=1, axis2=2)
    inverse_f = leaf_inverse.astype(jnp.float32)
    masked_f = masked.astype(jnp.float32)
    leaf_solve = jnp.einsum("lnm,lm->ln", inverse_f, leaf_rhs, precision=highest)
    leaf_terms = jnp.einsum("lnc,ln->lc", masked_f, leaf_solve, precision=highest)
    rhs_terms = jnp.dot(member_f.T, leaf_terms, precision=highest)
    rhs_sum, diag_sum = lax.psum((rhs_terms, diag_terms), "scen")
    reduced = node_rhs - rhs_sum
    scaling = node_diag + diag_sum
    schur_rows = lax.psum_scatter(partial_value, "scen", scatter_dimension=1, tiled=True)
    schur_out = lax.all_to_all(schur_rows, "scen", split_axis=2, concat_axis=1, tiled=True)
    row_count = schur_rows.shape[1]

    def own_rows(values):
        return lax.dynamic_slice_in_dim(values, scen_index * row_count, row_count, 1)

    reduced_own = own_rows(reduced)
    scaling_own = own_rows(scaling)
    diag_own = own_rows(node_diag)

    def assemble(portion):
        gathered = lax.all_gather(portion, ("scen", "blk"), axis=1, tiled=True)
        gathered = gathered.reshape(node_count, scen_count, blk_count, row_count)
        return gathered.transpose(0, 2, 1, 3).reshape(node_count, full_width)

    portion = reduced_own / scaling_own
    for sweep in range(ITERS):
        entire = assemble(portion)
        product = diag_own * portion + jnp.einsum(
            "prc,pc->pr", schur_rows, entire, precision=highest
        )
        portion = portion + damping * (reduced_own - product) / scaling_own
    node_solution = lax.dynamic_slice_in_dim(
        assemble(portion), blk_index * tile_width, tile_width, 1
    )
    parent_values = jnp.dot(member_f, node_solution, precision=highest)
    link_term = jnp.einsum("lnc,lc->ln", masked_f, parent_values, precision=highest)
    summed = lax.psum(link_term, "blk")
    leaf_solution = jnp.einsum("lnm,lm->ln", inverse_f, leaf_rhs - summed, precision=highest)
    return (node_solution, leaf_solution, schur_out)


def solution(mesh):
    in_specs = (
        P("scen", None, "blk"),
        P("scen", None, None),
        P("scen", None),
        P(None, "blk"),
        P(None, "blk"),
        P("scen"),
        P("scen", "blk"),
    )
    out_specs = (P(None, "blk"), P("scen", None), P(None, "blk", "scen"))
    return jax.shard_map(body, mesh=mesh, in_specs=in_specs, out_specs=out_specs, check_vma=False)
```

profile of v0, /device:TPU:1, one launch (start us, length us, event | category | flops | bytes accessed | tf_op | source)
XLA Modules:
  0.0 515.3 jit_solution(16813011652913458101)
XLA Ops:
  7.2 0.7 convert_bitcast_fusion
  7.9 1.1 broadcast_multiply_fusion
  9.1 1.1 fusion.5
  10.5 0.7 compare_convert_fusion
  11.2 59.3 %all-gather.7.cloned.1.call-done = bf16[4,256,4096]{1,2,0:T(8,128)(2,1)} async-done(((bf16[4,256,256]{1,2,0:T(8,128)(2,1)}), bf16[4,256,4096]{1,2,0:T(8,128)(2,1)}) %all-gather.7.cloned.1.call-update) | async-done | bytes 8388624 | tf_op jit(solution)/shard_map/all_gather | solution.py:28
  70.5 10.1 %fusion.2 = f32[2,256,4096]{2,1,0:T(8,128)} fusion(bf16[4,256,4096]{1,2,0:T(8,128)(2,1)} %all-gather.7.cloned.1.call-done, bf16[2,4]{1,0:T(2,128)(2,1)S(1)} %compare_convert_fusion, bf16[4,256,256]{1,2,0:T(8,128)(2,1)S(1)} %copy.43), kind=kOutput, calls=%fused_computation.3 | convolution fusion | flops 4295491584 | bytes 17301520 | tf_op jit(solution)/shard_map/pkr,kc->prc/dot_general | solution.py:30
  80.6 0.7 copy-done.2
  81.2 0.5 fusion.18
  82.4 1.1 constant_dynamic-slice_fusion.4
  83.5 16.4 %copy.46 = f32[2,256,256]{0,2,1:T(8,128)} copy(f32[2,256,256]{2,1,0:T(8,128)S(1)} %constant_dynamic-slice_fusion.4) | data formatting | bytes 1048576 | tf_op jit(solution)/shard_map/dynamic_slice | solution.py:31
  99.9 2.4 gather_fusion
  102.3 33.9 %all-reduce = (f32[2,256]{1,0:T(2,128)S(1)}, f32[2,256]{1,0:T(2,128)S(1)}) all-reduce(f32[2,256]{1,0:T(2,128)S(1)} %fusion.9, f32[2,256]{1,0:T(2,128)S(1)} %bitcast.136), channel_id=1, replica_groups=mesh['scen'=16,'blk'=16] {'scen'}, use_global_device_ids=true, to_apply=%region_0.1 | all-reduce | flops 1024 | bytes 8192 | tf_op jit(solution)/shard_map/psum | solution.py:38
  136.3 65.0 %all-gather = f32[256,16,2]{1,2,0:T(2,128)S(1)} all-gather(f32[1,16,2]{1,2,0:T(2,128)S(1)} %bitcast.132), channel_id=1, replica_groups=mesh['scen'=16,'blk'=16] {'scen','blk'}, dimensions={0}, use_global_device_ids=true | all-gather | bytes 32896 | tf_op jit(solution)/shard_map/all_gather | solution.py:53
  202.0 5.7 %copy.58 = f32[2,16,4096]{1,0,2:T(2,128)} copy(f32[2,16,4096]{2,1,0:T(8,128)} %reduce-scatter.2.cloned.1.call-done) | data formatting | bytes 1048576 | tf_op jit(solution)/shard_map/reduce_scatter | solution.py:41
  207.7 8.0 %reshape.107 = f32[16,1,8192]{2,1,0:T(1,128)} reshape(f32[4096,2,16]{2,1,0:T(2,128)} %bitcast.116) | data formatting | bytes 1048576
  215.6 5.3 %all-to-all-start = ((f32[16,1,8192]{2,1,0:T(1,128)}), f32[16,1,8192]{2,1,0:T(1,128)S(1)}, u32[]{:S(2)}, u32[]{:S(2)}) async-start(f32[16,1,8192]{2,1,0:T(1,128)} %reshape.107), calls=%async_computation.1 | async-start | bytes 1048576 | tf_op jit(solution)/shard_map/all_to_all | solution.py:42
  220.9 0.7 fusion.27
  221.7 62.9 %all-gather.1 = f32[256,16,2]{1,2,0:T(2,128)S(1)} all-gather(f32[1,16,2]{1,2,0:T(2,128)S(1)} %bitcast.134), channel_id=1, replica_groups=mesh['scen'=16,'blk'=16] {'scen','blk'}, dimensions={0}, use_global_device_ids=true | all-gather | bytes 32896 | tf_op jit(solution)/shard_map/all_gather | solution.py:53
  285.2 0.7 fusion.28
  286.0 59.3 %all-gather.2 = f32[256,16,2]{1,2,0:T(2,128)S(1)} all-gather(f32[1,16,2]{1,2,0:T(2,128)S(1)} %bitcast.135), channel_id=1, replica_groups=mesh['scen'=16,'blk'=16] {'scen','blk'}, dimensions={0}, use_global_device_ids=true | all-gather | bytes 32896 | tf_op jit(solution)/shard_map/all_gather | solution.py:53
  345.8 0.7 fusion.29
  346.6 59.8 %all-gather.3 = f32[256,16,2]{1,2,0:T(2,128)S(1)} all-gather(f32[1,16,2]{1,2,0:T(2,128)S(1)} %bitcast.133), channel_id=1, replica_groups=mesh['scen'=16,'blk'=16] {'scen','blk'}, dimensions={0}, use_global_device_ids=true | all-gather | bytes 32896 | tf_op jit(solution)/shard_map/all_gather | solution.py:53
  407.0 0.7 fusion.30
  407.8 59.6 %all-gather.4 = f32[256,16,2]{1,2,0:T(2,128)S(1)} all-gather(f32[1,16,2]{1,2,0:T(2,128)S(1)} %add_bitcast_fusion), channel_id=1, replica_groups=mesh['scen'=16,'blk'=16] {'scen','blk'}, dimensions={0}, use_global_device_ids=true | all-gather | bytes 32896 | tf_op jit(solution)/shard_map/all_gather | solution.py:53
  468.1 0.5 fusion.13
  468.7 23.1 %psum.23 = f32[4,256]{1,0:T(4,128)S(1)} all-reduce(f32[4,256]{1,0:T(4,128)S(1)} %bitcast.131), channel_id=1, replica_groups=mesh['scen'=16,'blk'=16] {'blk'}, use_global_device_ids=true, to_apply=%region_3.4 | all-reduce | flops 1024 | bytes 8192 | tf_op jit(solution)/shard_map/psum | solution.py:69
  491.7 0.5 fusion.11
  492.2 0.6 copy.103
  492.9 0.5 broadcast.39
  493.4 1.9 reduce
  495.3 6.9 %reshape.108 = f32[4096,2,16]{2,1,0:T(2,128)} reshape(f32[16,8192]{1,0:T(8,128)S(1)} %reduce) | data formatting | bytes 1048576
  502.2 6.3 %copy.59 = f32[2,16,16,256]{3,2,1,0:T(8,128)} copy(f32[2,16,16,256]{2,0,3,1:T(2,128)} %bitcast.115) | data formatting | bytes 1048576 | tf_op jit(solution)/shard_map/all_to_all | solution.py:42
  (59 shorter events, 4.3 us)
Async XLA Ops:
  7.2 1.9 copy-start
  7.2 63.3 %all-gather.7.cloned.1.call-start = ((), (), s32[]{:S(2)}) async-start(), calls=%async_computation.2 | async-start | bytes 8912896 | tf_op jit(solution)/shard_map/all_gather | solution.py:28
  10.3 191.7 %reduce-scatter.2.cloned.1.call-start = ((), (), s32[]{:S(2)}) async-start(), calls=%async_computation.3 | async-start | bytes 8912896 | tf_op jit(solution)/shard_map/reduce_scatter | solution.py:41
  80.6 0.7 copy-start.2
  80.6 1.5 copy-start.6
  83.4 52.8 %copy-start.3 = (f32[2,256]{1,0:T(2,128)S(1)}, f32[2,256]{1,0:T(2,128)}, u32[]{:S(2)}) copy-start(f32[2,256]{1,0:T(2,128)} %param.11) | copy-start | bytes 6148
  83.5 52.8 %copy-start.5 = (f32[2,256]{1,0:T(2,128)S(1)}, f32[2,256]{1,0:T(2,128)}, u32[]{:S(2)}) copy-start(f32[2,256]{1,0:T(2,128)} %param.10) | copy-start | bytes 6148
  202.0 19.0 %copy-start.1 = (f32[2,16,4096]{2,1,0:T(8,128)S(1)}, f32[2,16,4096]{2,1,0:T(8,128)}, u32[]{:S(2)}) copy-start(f32[2,16,4096]{2,1,0:T(8,128)} %reduce-scatter.2.cloned.1.call-done) | copy-start | bytes 1572868
  215.6 277.2 %all-to-all-start = ((f32[16,1,8192]{2,1,0:T(1,128)}), f32[16,1,8192]{2,1,0:T(1,128)S(1)}, u32[]{:S(2)}, u32[]{:S(2)}) async-start(f32[16,1,8192]{2,1,0:T(1,128)} %reshape.107), calls=%async_computation.1 | async-start | bytes 1048576 | tf_op jit(solution)/shard_map/all_to_all | solution.py:42
  468.0 40.5 %copy-start.4 = (f32[2,256]{1,0:T(2,128)}, f32[2,256]{1,0:T(2,128)S(1)}, u32[]{:S(2)}) copy-start(f32[2,256]{1,0:T(2,128)S(1)} %constant_dynamic-slice_fusion.1) | copy-start | bytes 6148
Sparse Core Ops, SparseCore 0:
  10.4 60.0 all-gather.6
  80.7 87.5 reduce-scatter.1
where the time goes:
time: 516 us; the launch traced here: 515 us
  blocking collectives  364 us (71%)
  waiting for transfers between devices  59.4 us (12%)
  local copies, waits for them, and re-layouts  51.5 us (10%)
  matrix products  16.2 us (3%)
  between operations  14.3 us (3%)
  starting transfers between devices  5.36 us (1%)
    all_gather x5, blocking collectives, assemble(): gathered = lax.all_gather(portion, ('scen', 'blk'), axis=1, tiled=True)  307 us
    all_gather x1, waiting for transfers between devices, body(): portion = lax.all_gather(solved, 'blk', axis=2, tiled=True)  59.3 us
    psum x1, blocking collectives, body(): rhs_sum, diag_sum = lax.psum((rhs_terms, diag_terms), 'scen')  33.9 us
    psum x1, blocking collectives, body(): summed = lax.psum(link_term, 'blk')  23.1 us
    dynamic_slice x2, local copies, waits for them, and re-layouts, body(): lax.dynamic_slice_in_dim(partial_value, blk_index * tile_width, tile_widt...  17.5 us
    unnamed x21, local copies, waits for them, and re-layouts  16.3 us
  transfers between devices with their start and end apart: 3, of which 1 were waited for; matrix products, arithmetic and copies ran while one was open for 6% of the time, Pallas kernels for 0%

commit v1 on v0

--- a/solution.py
+++ b/solution.py
@@ -25,7 +25,10 @@
     ).astype(jnp.bfloat16)
     chosen = masked[None] * member.astype(jnp.bfloat16).T[:, :, None, None]
     chosen = chosen.reshape(node_count, leaf_count * width_leaf, tile_width)
-    portion = lax.all_gather(solved, "blk", axis=2, tiled=True)
+    size = lax.axis_size("blk")
+    blocks = jnp.stack([solved for _ in range(size)])
+    blocks = lax.all_to_all(blocks, "blk", split_axis=0, concat_axis=0)
+    portion = jnp.concatenate(blocks, axis=2)
     stacked = portion.reshape(leaf_count * width_leaf, portion.shape[2])
     partial_value = jnp.einsum("pkr,kc->prc", chosen, stacked, preferred_element_type=jnp.float32)
     diagonal_tile = lax.dynamic_slice_in_dim(partial_value, blk_index * tile_width, tile_width, 2)

time: 516 us -> 680 us (1.32)
  waiting for transfers between devices: 59.4 us -> 183 us
  local copies, waits for them, and re-layouts: 51.5 us -> 81.4 us
  starting transfers between devices: 5.36 us -> 15.4 us
    all_to_all x0 -> x1, waiting for transfers between devices: none -> 183 us  [body(): blocks = lax.all_to_all(blocks, 'blk', split_axis=0, concat_axis=0)]
    all_gather x1 -> x0, waiting for transfers between devices: 59.3 us -> none  [body(): portion = lax.all_gather(solved, 'blk', axis=2, tiled=True)]
    another operation x0 -> x2, local copies, waits for them, and re-layouts: none -> 17.7 us  [the longest x1 13.5 us: body(): stacked = portion.reshape(leaf_count * width_leaf, portion.shape[2])]
    reshape x0 -> x1, local copies, waits for them, and re-layouts: none -> 11.5 us  [body(): portion = jnp.concatenate(blocks, axis=2)]
    all_to_all x0 -> x1, starting transfers between devices: none -> 10.1 us  [body(): blocks = lax.all_to_all(blocks, 'blk', split_axis=0, concat_axis=0)]
    unnamed x21 -> x23, local copies, waits for them, and re-layouts: 16.3 us -> 16.4 us
  transfers between devices with their start and end apart: 3 -> 3, of which waited for: 1 -> 1; matrix products, arithmetic and copies ran while one was open for 6% -> 4% of each run, Pallas kernels for 0% -> 0%
where the time goes in v1:
time: 680 us; the launch traced here: 679 us
  blocking collectives  365 us (54%)
  waiting for transfers between devices  183 us (27%)
  local copies, waits for them, and re-layouts  81.4 us (12%)
  matrix products  15.4 us (2%)
  starting transfers between devices  15.4 us (2%)
  between operations  14.3 us (2%)
    all_gather x5, blocking collectives, assemble(): gathered = lax.all_gather(portion, ('scen', 'blk'), axis=1, tiled=True)  308 us
    all_to_all x1, waiting for transfers between devices, body(): blocks = lax.all_to_all(blocks, 'blk', split_axis=0, concat_axis=0)  183 us
    psum x1, blocking collectives, body(): rhs_sum, diag_sum = lax.psum((rhs_terms, diag_terms), 'scen')  34.3 us
    psum x1, blocking collectives, body(): summed = lax.psum(link_term, 'blk')  23.1 us
    dynamic_slice x2, local copies, waits for them, and re-layouts, body(): lax.dynamic_slice_in_dim(partial_value, blk_index * tile_width, tile_widt...  17.9 us
    unnamed x23, local copies, waits for them, and re-layouts  16.4 us
  transfers between devices with their start and end apart: 3, of which 1 were waited for; matrix products, arithmetic and copies ran while one was open for 4% of the time, Pallas kernels for 0%

profile of v1, /device:TPU:1, one launch (start us, length us, event | category | flops | bytes accessed | tf_op | source)
XLA Modules:
  0.0 678.8 jit_solution(16859222408671119022)
XLA Ops:
  7.2 0.7 convert_bitcast_fusion
  7.9 1.1 broadcast_multiply_fusion
  9.6 4.2 stack.2
  13.8 10.1 %all-to-all-start = ((bf16[16,4,256,256]{3,2,1,0:T(8,128)(2,1)}), bf16[16,4,256,256]{3,2,1,0:T(8,128)(2,1)}, u32[]{:S(2)}, u32[]{:S(2)}) async-start(bf16[16,4,256,256]{3,2,1,0:T(8,128)(2,1)} %stack.2), calls=%async_computation | async-start | bytes 16777216 | tf_op jit(solution)/shard_map/all_to_all | solution.py:30
  24.3 183.0 %all-to-all-done = bf16[16,4,256,256]{3,2,1,0:T(8,128)(2,1)} async-done(((bf16[16,4,256,256]{3,2,1,0:T(8,128)(2,1)}), bf16[16,4,256,256]{3,2,1,0:T(8,128)(2,1)}, u32[]{:S(2)}, u32[]{:S(2)}) %all-to-all-start) | async-done | bytes 8388640 | tf_op jit(solution)/shard_map/all_to_all | solution.py:30
  207.3 11.5 %copy.50 = bf16[4,256,16,256]{3,2,1,0:T(8,128)(2,1)} copy(bf16[4,256,16,256]{3,1,0,2:T(8,128)(2,1)} %bitcast.7) | data formatting | bytes 16777216 | tf_op jit(solution)/shard_map/reshape | solution.py:31
  218.8 13.5 %reshape.93 = bf16[1024,4096,1]{1,0,2:T(8,128)(2,1)} reshape(bf16[4,256,16,256]{3,2,1,0:T(8,128)(2,1)} %copy.50) | data formatting | bytes 16777216 | tf_op jit(solution)/shard_map/reshape;reshape | solution.py:32
  232.3 10.0 %fusion.1 = f32[2,256,4096]{2,1,0:T(8,128)} fusion(bf16[1024,4096,1]{1,0,2:T(8,128)(2,1)} %reshape.93, bf16[2,1024]{1,0:T(2,128)(2,1)S(1)} %bitcast.143, bf16[1024,256]{0,1:T(8,128)(2,1)S(1)} %copy.47), kind=kOutput, calls=%fused_computation.4 | convolution fusion | flops 4295491584 | bytes 17305600 | tf_op jit(solution)/shard_map/pkr,kc->prc/dot_general | solution.py:33
  242.3 0.7 copy-done.2
  244.1 1.1 constant_dynamic-slice_fusion.4
  245.2 16.8 %copy.51 = f32[2,256,256]{0,2,1:T(8,128)} copy(f32[2,256,256]{2,1,0:T(8,128)S(1)} %constant_dynamic-slice_fusion.4) | data formatting | bytes 1048576 | tf_op jit(solution)/shard_map/dynamic_slice | solution.py:34
  262.1 2.4 gather_fusion
  264.5 34.3 %all-reduce = (f32[2,256]{1,0:T(2,128)S(1)}, f32[2,256]{1,0:T(2,128)S(1)}) all-reduce(f32[2,256]{1,0:T(2,128)S(1)} %fusion.5, f32[2,256]{1,0:T(2,128)S(1)} %bitcast.137), channel_id=1, replica_groups=mesh['scen'=16,'blk'=16] {'scen'}, use_global_device_ids=true, to_apply=%region_0.1 | all-reduce | flops 1024 | bytes 8192 | tf_op jit(solution)/shard_map/psum | solution.py:41
  298.9 65.9 %all-gather = f32[256,16,2]{1,2,0:T(2,128)S(1)} all-gather(f32[1,16,2]{1,2,0:T(2,128)S(1)} %bitcast.133), channel_id=1, replica_groups=mesh['scen'=16,'blk'=16] {'scen','blk'}, dimensions={0}, use_global_device_ids=true | all-gather | bytes 32896 | tf_op jit(solution)/shard_map/all_gather | solution.py:56
  365.5 5.7 copy.63
  371.2 8.0 %reshape.115 = f32[16,1,8192]{2,1,0:T(1,128)} reshape(f32[4096,2,16]{2,1,0:T(2,128)} %bitcast.116) | data formatting | bytes 1048576
  379.1 5.3 all-to-all-start.1
  384.4 0.7 fusion.23
  385.2 62.4 %all-gather.1 = f32[256,16,2]{1,2,0:T(2,128)S(1)} all-gather(f32[1,16,2]{1,2,0:T(2,128)S(1)} %bitcast.135), channel_id=1, replica_groups=mesh['scen'=16,'blk'=16] {'scen','blk'}, dimensions={0}, use_global_device_ids=true | all-gather | bytes 32896 | tf_op jit(solution)/shard_map/all_gather | solution.py:56
  448.2 0.7 fusion.24
  448.9 59.8 %all-gather.2 = f32[256,16,2]{1,2,0:T(2,128)S(1)} all-gather(f32[1,16,2]{1,2,0:T(2,128)S(1)} %bitcast.136), channel_id=1, replica_groups=mesh['scen'=16,'blk'=16] {'scen','blk'}, dimensions={0}, use_global_device_ids=true | all-gather | bytes 32896 | tf_op jit(solution)/shard_map/all_gather | solution.py:56
  509.3 0.7 fusion.25
  510.1 59.6 %all-gather.3 = f32[256,16,2]{1,2,0:T(2,128)S(1)} all-gather(f32[1,16,2]{1,2,0:T(2,128)S(1)} %bitcast.134), channel_id=1, replica_groups=mesh['scen'=16,'blk'=16] {'scen','blk'}, dimensions={0}, use_global_device_ids=true | all-gather | bytes 32896 | tf_op jit(solution)/shard_map/all_gather | solution.py:56
  570.3 0.7 fusion.26
  571.0 59.8 %all-gather.4 = f32[256,16,2]{1,2,0:T(2,128)S(1)} all-gather(f32[1,16,2]{1,2,0:T(2,128)S(1)} %add_bitcast_fusion), channel_id=1, replica_groups=mesh['scen'=16,'blk'=16] {'scen','blk'}, dimensions={0}, use_global_device_ids=true | all-gather | bytes 32896 | tf_op jit(solution)/shard_map/all_gather | solution.py:56
  631.6 0.5 fusion.9
  632.2 23.1 %psum.23 = f32[4,256]{1,0:T(4,128)S(1)} all-reduce(f32[4,256]{1,0:T(4,128)S(1)} %bitcast.132), channel_id=1, replica_groups=mesh['scen'=16,'blk'=16] {'blk'}, use_global_device_ids=true, to_apply=%region_3.4 | all-reduce | flops 1024 | bytes 8192 | tf_op jit(solution)/shard_map/psum | solution.py:72
  655.7 0.6 copy.106
  656.3 0.5 broadcast.43
  656.9 1.9 reduce
  658.8 6.9 %reshape.116 = f32[4096,2,16]{2,1,0:T(2,128)} reshape(f32[16,8192]{1,0:T(8,128)S(1)} %reduce) | data formatting | bytes 1048576
  665.7 6.3 copy.64
  (64 shorter events, 5.9 us)
Async XLA Ops:
  7.2 1.9 copy-start
  13.8 10.2 %copy-start.6 = (s32[4]{0:T(128)S(1)}, s32[4]{0:T(128)}, u32[]{:S(2)}) copy-start(s32[4]{0:T(128)} %param.12) | copy-start | bytes 52
  13.8 193.5 %all-to-all-start = ((bf16[16,4,256,256]{3,2,1,0:T(8,128)(2,1)}), bf16[16,4,256,256]{3,2,1,0:T(8,128)(2,1)}, u32[]{:S(2)}, u32[]{:S(2)}) async-start(bf16[16,4,256,256]{3,2,1,0:T(8,128)(2,1)} %stack.2), calls=%async_computation | async-start | bytes 16777216 | tf_op jit(solution)/shard_map/all_to_all | solution.py:30
  24.0 341.5 %reduce-scatter.2.cloned.1.call-start = ((), (), s32[]{:S(2)}) async-start(), calls=%async_computation.3 | async-start | bytes 8912896 | tf_op jit(solution)/shard_map/reduce_scatter | solution.py:44
  242.3 0.7 copy-start.2
  245.2 53.7 %copy-start.3 = (f32[2,256]{1,0:T(2,128)S(1)}, f32[2,256]{1,0:T(2,128)}, u32[]{:S(2)}) copy-start(f32[2,256]{1,0:T(2,128)} %param.11) | copy-start | bytes 6148
  245.2 53.6 %copy-start.5 = (f32[2,256]{1,0:T(2,128)S(1)}, f32[2,256]{1,0:T(2,128)}, u32[]{:S(2)}) copy-start(f32[2,256]{1,0:T(2,128)} %param.10) | copy-start | bytes 6148
  365.4 19.0 %copy-start.1 = (f32[2,16,4096]{2,1,0:T(8,128)S(1)}, f32[2,16,4096]{2,1,0:T(8,128)}, u32[]{:S(2)}) copy-start(f32[2,16,4096]{2,1,0:T(8,128)} %reduce-scatter.2.cloned.1.call-done) | copy-start | bytes 1572868
  379.1 277.2 %all-to-all-start.1 = ((f32[16,1,8192]{2,1,0:T(1,128)}), f32[16,1,8192]{2,1,0:T(1,128)S(1)}, u32[]{:S(2)}, u32[]{:S(2)}) async-start(f32[16,1,8192]{2,1,0:T(1,128)} %reshape.115), calls=%async_computation.2 | async-start | bytes 1048576 | tf_op jit(solution)/shard_map/all_to_all | solution.py:45
  631.4 40.5 %copy-start.4 = (f32[2,256]{1,0:T(2,128)}, f32[2,256]{1,0:T(2,128)S(1)}, u32[]{:S(2)}) copy-start(f32[2,256]{1,0:T(2,128)S(1)} %constant_dynamic-slice_fusion.1) | copy-start | bytes 6148
Sparse Core Ops, SparseCore 0:
  242.5 88.8 reduce-scatter.1
